TPU v7x, 128 devices: a whole 4x4x4 slice. The times are simulated.
128 devices in a mesh: dom: 16 (over x, y), blk: 8 (over z, core).
Axes of the slice: x: 4, y: 4, z: 4, core: 2. Of those that a mesh axis runs over, the one named last changes fastest.
Arguments:
- node_features: bfloat16 [32768, 512], P(('dom', 'blk')), may hold values from -6 to 6
- norm_gain: float32 [512], replicated, may hold values from 0.25 to 1.75
- w_query: bfloat16 [512, 512], replicated, may hold values from -0.25 to 0.25
- w_key: bfloat16 [512, 512], replicated, may hold values from -0.25 to 0.25
- w_value: bfloat16 [512, 512], replicated, may hold values from -0.25 to 0.25
- w_out: bfloat16 [512, 512], replicated, may hold values from -1.5 to 1.5
- w_message: bfloat16 [512, 512], replicated, may hold values from -1 to 1
- node_cluster: int32 [32768], P(('dom', 'blk')), may hold values from 0 to 15
- block_pattern: int32 [128, 8], P(('dom', 'blk')), may hold values from 0 to 1, as said below
- send_rows: int32 [2048, 128], P(('dom', 'blk')), may hold values from 0 to 255
- send_counts: int32 [2048], P(('dom', 'blk')), may hold values from 32 to 128, as said below
- edge_src: int32 [524288], P(('dom', 'blk')), may hold values from 0 to 2047
- edge_dst: int32 [524288], P(('dom', 'blk')), may hold values from 0 to 255
- out_grad: bfloat16 [32768, 512], P(('dom', 'blk')), may hold values from -6 to 6
Outputs:
- layer_out: bfloat16 [32768, 512], P(('dom', 'blk'))
- feature_grad: bfloat16 [32768, 512], P(('dom', 'blk'))
- weight_grads: float32 [5, 512, 512], replicated
- gain_grad: float32 [512], replicated
Inputs may be any that keep to these rules, and one draw needn't show every extreme that they name: `block_pattern`: row g has a 1 at column (g mod 8); other entries are 0 or 1. `send_counts`: entry g * 16 + p is how many leading slots of device g's block to dom peer p are live; every device has one peer whose block has all 128 slots live.
All inputs are finite; a program needn't handle non-finite values.
Results may differ from a plain program's by a relative error of at most 0.013.
Values may be sent and summed in bfloat16 or wider, within the bound.
No kernel may reach another device: no remote copies, remote signals or barrier semaphores. Data moves between devices by JAX's collectives and lax.ppermute only.
A program may use at most 128 MiB of HBM per device.

v0:
```python
from functools import partial
import jax
import jax.numpy as jnp
from jax import lax
from jax.sharding import PartitionSpec as P

HEADS = 8
HEAD_DIM = 64
epsilon = 1e-06
score_shift = 8.0


def settle(array):
    return lax.optimization_barrier(array.astype(jnp.bfloat16)).astype(jnp.float32)


def rms_norm(features, norm_gain):
    scaling = lax.rsqrt(jnp.mean(features * features, axis=-1, keepdims=True) + epsilon)
    return features * scaling * norm_gain


def head_norm(projected):
    head_view = projected.reshape(projected.shape[0], HEADS, HEAD_DIM)
    scaling = lax.rsqrt(jnp.mean(head_view * head_view, axis=-1, keepdims=True) + epsilon)
    return (head_view * scaling).reshape(projected.shape)


def block_weights(query_heads, key_heads, allowed):
    scaling = score_shift / HEAD_DIM
    scores = (
        jnp.einsum("rhe,khe->hrk", query_heads, key_heads, preferred_element_type=jnp.float32)
        * scaling
    )
    return jnp.where(allowed[None], jnp.exp(scores - score_shift), 0.0)


def attend_piece(running, shard_piece, offset, query_heads, query_labels, pattern_row, skip_empty):
    key_rows, value_rows, key_labels = shard_piece
    row_count = query_heads.shape[0]
    piece_rows = key_rows.shape[0]
    part_count = max(piece_rows // row_count, 1)
    block_index = jnp.arange(pattern_row.shape[0], dtype=jnp.int32)
    for position in range(part_count):
        first_row = position * piece_rows // part_count
        last_row = (position + 1) * piece_rows // part_count
        part_rows = last_row - first_row
        key_part = key_rows[first_row:last_row].reshape(part_rows, HEADS, HEAD_DIM)
        value_part = value_rows[first_row:last_row].reshape(part_rows, HEADS, HEAD_DIM)
        label_part = key_labels[first_row:last_row]
        owners = (offset + first_row + jnp.arange(part_rows, dtype=jnp.int32)) // row_count
        block_flags = jnp.sum(
            jnp.where(owners[:, None] == block_index[None, :], pattern_row[None, :], 0), axis=1
        )
        allowed = (query_labels[:, None] == label_part[None, :]) & (block_flags[None, :] == 1)

        def accumulate(current, key_part=key_part, value_part=value_part, allowed=allowed):
            numer, denom = current
            weights = block_weights(query_heads, key_part, allowed)
            denom = denom + jnp.sum(weights, axis=2).T
            numer = numer + jnp.einsum(
                "hrk,khe->rhe",
                weights.astype(jnp.bfloat16),
                value_part,
                preferred_element_type=jnp.float32,
            )
            return (numer, denom)

        running = accumulate(running)
    return running


def pair_gradients(query_heads, grad_heads, correction, key_part, value_part, allowed):
    scaling = score_shift / HEAD_DIM
    weights = block_weights(query_heads, key_part, allowed)
    grad_dots = jnp.einsum(
        "rhe,khe->hrk", grad_heads, value_part, preferred_element_type=jnp.float32
    )
    slopes = (weights * (grad_dots - correction.T[:, :, None])).astype(jnp.bfloat16)
    dq_part = (
        jnp.einsum("hrk,khe->rhe", slopes, key_part, preferred_element_type=jnp.float32) * scaling
    )
    dk_part = (
        jnp.einsum("hrk,rhe->khe", slopes, query_heads, preferred_element_type=jnp.float32)
        * scaling
    )
    dv_part = jnp.einsum(
        "hrk,rhe->khe", weights.astype(jnp.bfloat16), grad_heads, preferred_element_type=jnp.float32
    )
    return (dq_part, dk_part, dv_part)


def key_block(
    query_heads, grad_heads, correction, query_labels, skip_empty, dq_total, block_inputs
):
    key_part, value_part, label_part, block_flag = block_inputs
    row_count = query_heads.shape[0]
    allowed = (query_labels[:, None] == label_part[None, :]) & (block_flag == 1)
    dq_part, dk_part, dv_part = pair_gradients(
        query_heads, grad_heads, correction, key_part, value_part, allowed
    )
    flat_terms = (dk_part.reshape(row_count, -1), dv_part.reshape(row_count, -1))
    return (dq_total + settle(dq_part), flat_terms)


def local(
    node_features,
    norm_gain,
    w_query,
    w_key,
    w_value,
    w_out,
    w_message,
    node_cluster,
    block_pattern,
    send_rows,
    send_counts,
    edge_src,
    edge_dst,
    out_grad,
):
    row_count = node_features.shape[0]
    feat_width = node_features.shape[1]
    peer_count = lax.axis_size("dom")
    block_count = lax.axis_size("blk")
    slot_count = send_rows.shape[1]
    features = node_features.astype(jnp.float32)
    normed_f, norm_pull = jax.vjp(rms_norm, features, norm_gain)
    normed = normed_f.astype(jnp.bfloat16)
    live_slots = jnp.arange(slot_count, dtype=jnp.int32)[None, :] < send_counts[:, None]
    outgoing = jnp.where(live_slots[:, :, None], normed[send_rows], jnp.zeros((), jnp.bfloat16))
    incoming = lax.all_to_all(outgoing, "dom", split_axis=0, concat_axis=0, tiled=True)
    query_f, query_pull = jax.vjp(
        head_norm, jnp.dot(normed, w_query, preferred_element_type=jnp.float32)
    )
    key_f, key_pull = jax.vjp(head_norm, jnp.dot(normed, w_key, preferred_element_type=jnp.float32))
    queries = query_f.astype(jnp.bfloat16)
    key_flat = key_f.astype(jnp.bfloat16)
    value_flat = jnp.dot(normed, w_value, preferred_element_type=jnp.float32).astype(jnp.bfloat16)
    query_heads = queries.reshape(row_count, HEADS, HEAD_DIM)
    pattern_row = block_pattern[0]
    start_state = (
        jnp.zeros((row_count, HEADS, HEAD_DIM), jnp.float32),
        jnp.zeros((row_count, HEADS), jnp.float32),
    )
    fold_step = partial(
        attend_piece,
        query_heads=query_heads,
        query_labels=node_cluster,
        pattern_row=pattern_row,
        skip_empty=False,
    )
    key_set = None
    key_set = (
        lax.all_gather(key_flat, "blk", axis=0, tiled=True),
        lax.all_gather(value_flat, "blk", axis=0, tiled=True),
        lax.all_gather(node_cluster, "blk", axis=0, tiled=True),
    )
    numer, denom = fold_step(start_state, key_set, 0)
    slot_table = incoming.reshape(peer_count * slot_count, feat_width)
    pair_index = edge_src * row_count + edge_dst
    edge_counts = jnp.zeros((peer_count * slot_count * row_count,), jnp.int32).at[pair_index].add(1)
    edge_counts = edge_counts.reshape(peer_count * slot_count, row_count).astype(jnp.bfloat16)
    degree = jnp.maximum(
        jax.ops.segment_sum(jnp.ones(edge_dst.shape, jnp.float32), edge_dst, row_count), 1.0
    )
    neighbour_sum = jnp.einsum(
        "sr,sd->rd", edge_counts, slot_table, preferred_element_type=jnp.float32
    )
    mean_rows = (neighbour_sum / degree[:, None]).astype(jnp.bfloat16)
    local_term = jnp.dot(mean_rows, w_message, preferred_element_type=jnp.float32)
    attn_heads = (numer / denom[..., None]).astype(jnp.bfloat16)
    attn_rows = attn_heads.reshape(row_count, feat_width)
    attn_proj = jnp.dot(attn_rows, w_out, preferred_element_type=jnp.float32)
    layer_out = (features + local_term + attn_proj).astype(jnp.bfloat16)
    grad_attn = jnp.einsum(
        "rd,ed->re", out_grad, w_out, preferred_element_type=jnp.float32
    ).reshape(row_count, HEADS, HEAD_DIM)
    grad_heads = (grad_attn / denom[..., None]).astype(jnp.bfloat16)
    correction = jnp.sum(grad_attn * attn_heads.astype(jnp.float32), axis=-1) / denom
    key_rows, value_rows, key_labels = key_set
    block_inputs = (
        key_rows.reshape(block_count, row_count, HEADS, HEAD_DIM),
        value_rows.reshape(block_count, row_count, HEADS, HEAD_DIM),
        key_labels.reshape(block_count, row_count),
        pattern_row,
    )
    block_step = partial(key_block, query_heads, grad_heads, correction, node_cluster, False)
    dq_heads, (key_terms, value_terms) = lax.scan(
        block_step, jnp.zeros((row_count, HEADS, HEAD_DIM), jnp.float32), block_inputs
    )
    key_grad, value_grad = (
        lax.psum_scatter(
            key_terms.reshape(block_count * row_count, feat_width).astype(jnp.bfloat16),
            "blk",
            scatter_dimension=0,
            tiled=True,
        ).astype(jnp.float32),
        lax.psum_scatter(
            value_terms.reshape(block_count * row_count, feat_width).astype(jnp.bfloat16),
            "blk",
            scatter_dimension=0,
            tiled=True,
        ).astype(jnp.float32),
    )
    dq_flat = dq_heads.reshape(row_count, feat_width)
    dquery = query_pull(dq_flat)[0].astype(jnp.bfloat16)
    dkey = key_pull(key_grad)[0].astype(jnp.bfloat16)
    dvalue = value_grad.astype(jnp.bfloat16)
    dmessage = (
        jnp.einsum("rd,ed->re", out_grad, w_message, preferred_element_type=jnp.float32)
        / degree[:, None]
    ).astype(jnp.bfloat16)
    slot_grads = jnp.dot(edge_counts, dmessage, preferred_element_type=jnp.float32).astype(
        jnp.bfloat16
    )
    returned = lax.all_to_all(
        slot_grads.reshape(peer_count, slot_count, feat_width),
        "dom",
        split_axis=0,
        concat_axis=0,
        tiled=True,
    )
    returned = jnp.where(live_slots[:, :, None], returned.astype(jnp.float32), 0.0)
    halo_grad = jax.ops.segment_sum(
        returned.reshape(peer_count * slot_count, feat_width), send_rows.reshape(-1), row_count
    )
    dnormed = jnp.einsum("rd,ed->re", dquery, w_query, preferred_element_type=jnp.float32)
    dnormed = dnormed + jnp.einsum("rd,ed->re", dkey, w_key, preferred_element_type=jnp.float32)
    dnormed = dnormed + jnp.einsum("rd,ed->re", dvalue, w_value, preferred_element_type=jnp.float32)
    dnormed = dnormed + halo_grad
    dfeatures, gain_term = norm_pull(dnormed)
    feature_grad = (out_grad.astype(jnp.float32) + dfeatures).astype(jnp.bfloat16)
    weight_terms = jnp.stack(
        [
            jnp.einsum("rd,re->de", normed, dquery, preferred_element_type=jnp.float32),
            jnp.einsum("rd,re->de", normed, dkey, preferred_element_type=jnp.float32),
            jnp.einsum("rd,re->de", normed, dvalue, preferred_element_type=jnp.float32),
            jnp.einsum("rd,re->de", attn_rows, out_grad, preferred_element_type=jnp.float32),
            jnp.einsum("rd,re->de", mean_rows, out_grad, preferred_element_type=jnp.float32),
        ]
    )
    weight_sums, gain_sum = lax.psum((weight_terms, gain_term), ("dom", "blk"))
    return (layer_out, feature_grad, weight_sums, gain_sum)


def solution(mesh):
    placed = (
        P(("dom", "blk"), None),
        P(),
        P(),
        P(),
        P(),
        P(),
        P(),
        P(("dom", "blk")),
        P(("dom", "blk"), None),
        P(("dom", "blk"), None),
        P(("dom", "blk")),
        P(("dom", "blk")),
        P(("dom", "blk")),
        P(("dom", "blk"), None),
    )
    return jax.shard_map(
        local,
        mesh=mesh,
        in_specs=placed,
        out_specs=(P(("dom", "blk"), None), P(("dom", "blk"), None), P(), P()),
        check_vma=False,
    )
```

profile of v0, /device:TPU:1, one launch (start us, length us, event | category | flops | bytes accessed | tf_op | source)
XLA Modules:
  0.0 467.6 jit_solution(4525256311109926087)
XLA Ops:
  9.5 1.3 fusion.57
  15.0 2.1 copy.152
  18.3 13.1 %all-gather = s32[8,1,256]{2,1,0:T(1,128)S(1)} all-gather(s32[1,1,256]{2,1,0:T(1,128)S(1)} %bitcast.258), channel_id=1, replica_groups=mesh['dom'=16,'blk'=8] {'blk'}, dimensions={0}, use_global_device_ids=true | all-gather | bytes 9216 | tf_op jit(solution)/shard_map/all_gather | solution.py:156
  31.7 1.5 compare_and_fusion.1
  33.6 7.9 %all-gather.6.cloned.1.call-done = bf16[2048,512]{1,0:T(8,128)(2,1)} async-done(((bf16[256,512]{1,0:T(8,128)(2,1)}), bf16[2048,512]{1,0:T(8,128)(2,1)}) %all-gather.6.cloned.1.call-update) | async-done | bytes 2097168 | tf_op jit(solution)/shard_map/all_gather | solution.py:154
  41.5 2.5 fusion.54
  43.9 1.8 copy.156
  45.7 23.3 %all-gather.4.cloned.1.call-done = bf16[2048,512]{1,0:T(8,128)(2,1)} async-done(((bf16[256,512]{1,0:T(8,128)(2,1)}), bf16[2048,512]{1,0:T(8,128)(2,1)}) %all-gather.4.cloned.1.call-update) | async-done | bytes 2097168 | tf_op jit(solution)/shard_map/all_gather | solution.py:155
  69.0 2.8 fusion.55
  71.9 1.8 copy.150
  83.3 1.8 copy.174
  85.1 1.8 copy.173
  86.9 1.8 copy.177
  88.7 1.8 copy.176
  90.5 1.8 fusion.64
  101.9 6.1 %reshape.794 = bf16[8,256,8,64]{3,2,1,0:T(8,128)(2,1)} reshape(bf16[2048,512]{1,0:T(8,128)(2,1)} %all-gather.6.cloned.1.call-done) | data formatting | bytes 4194304 | tf_op jit(solution)/shard_map/reshape | solution.py:182
  108.0 5.1 %copy.182 = bf16[8,256,8,64]{1,3,2,0:T(8,128)(2,1)} copy(bf16[8,256,8,64]{3,2,1,0:T(8,128)(2,1)} %reshape.794) | data formatting | bytes 4194304
  113.1 6.1 %reshape.795 = bf16[8,256,8,64]{3,2,1,0:T(8,128)(2,1)} reshape(bf16[2048,512]{1,0:T(8,128)(2,1)} %all-gather.4.cloned.1.call-done) | data formatting | bytes 4194304 | tf_op jit(solution)/shard_map/reshape | solution.py:183
  119.3 5.1 %copy.183 = bf16[8,256,8,64]{1,3,2,0:T(8,128)(2,1)} copy(bf16[8,256,8,64]{3,2,1,0:T(8,128)(2,1)} %reshape.795) | data formatting | bytes 4194304
  124.4 67.0 %while.17 = (s32[]{:T(128)}, f32[256,8,64]{0,2,1:T(8,128)S(1)}, bf16[8,256,512]{1,2,0:T(8,128)(2,1)}, bf16[8,256,512]{2,1,0:T(8,128)(2,1)}, bf16[8,256,8,64]{1,3...) while((s32[]{:T(128)}, f32[256,8,64]{0,2,1:T(8,128)S(1)}, ...), condition=%wide.region_23.24_spmd.clone, body=%wide.region_22.23_spmd.clone.sunk | while | flops 340262912 | bytes 15088305 | solution.py:188
  125.8 1.6 bitcast_select_fusion.2
  127.4 1.4 fusion.163
  134.1 1.6 bitcast_select_fusion.2
  135.7 1.4 fusion.163
  142.5 1.6 bitcast_select_fusion.2
  144.1 1.4 fusion.163
  148.0 1.2 fusion.164
  150.9 1.6 bitcast_select_fusion.2
  152.5 1.4 fusion.163
  159.2 1.6 bitcast_select_fusion.2
  160.8 1.4 fusion.163
  164.8 1.2 fusion.164
  167.6 1.6 bitcast_select_fusion.2
  169.2 1.4 fusion.163
  176.0 1.6 bitcast_select_fusion.2
  177.6 1.4 fusion.163
  184.4 1.6 bitcast_select_fusion.2
  186.0 1.4 fusion.163
  189.9 1.2 fusion.164
  191.4 4.0 copy.184
  196.1 7.5 %gather_fusion = bf16[2048,512]{1,0:T(8,128)(2,1)S(1)} fusion(bf16[256,512]{1,0:T(8,128)(2,1)S(1)} %fusion.38, s32[2048]{0:T(1024)S(1)} %fusion.48), kind=kCustom, calls=%fused_computation | custom fusion | bytes 4202496 | tf_op jit(solution)/shard_map/gather | solution.py:130
  203.7 1.5 broadcast_select_fusion
  205.2 6.6 %all-to-all-start = ((bf16[16,128,512]{2,1,0:T(8,128)(2,1)}), bf16[16,128,512]{2,1,0:T(8,128)(2,1)}, u32[]{:S(2)}, u32[]{:S(2)}) async-start(bf16[16,128,512]{2,1,0:T(8,128)(2,1)} %broadcast_select_fusion), calls=%async_computation | async-start | bytes 4194304 | tf_op jit(solution)/shard_map/all_to_all | solution.py:131
  212.6 22.4 %scatter_custom_fusion = s32[524288]{0:T(1024)S(1)} fusion(s32[4096]{0:T(1024)S(1)} %compare_select_fusion, s32[4096]{0:T(1024)S(1)} %broadcast.736, s32[]{:T(128)} %constant.148.clone.1), kind=kCustom, calls=%fused_computation.77 | custom fusion | flops 4096 | bytes 2097156 | tf_op jit(solution)/shard_map/scatter-add | solution.py:161
  236.1 1.5 convert_element_type.131
  237.6 28.8 %scatter_custom_fusion.1 = f32[256]{0:T(256)S(1)} fusion(s32[4096]{0:T(1024)S(1)} %copy-done.48, f32[4096]{0:T(1024)S(1)} %broadcast.737, f32[]{:T(128)} %constant.152.clone.1), kind=kCustom, calls=%fused_computation.188 | custom fusion | flops 4096 | bytes 1028 | tf_op jit(solution)/shard_map/scatter-add | solution.py:164
  266.4 2.4 convolution_convert_fusion
  268.8 6.6 %all-to-all-start.1 = ((bf16[16,128,512]{2,1,0:T(8,128)(2,1)}), bf16[16,128,512]{2,1,0:T(8,128)(2,1)S(1)}, u32[]{:S(2)}, u32[]{:S(2)}) async-start(bf16[16,128,512]{2,1,0:T(8,128)(2,1)} %bitcast.233), calls=%async_computation.3 | async-start | bytes 4194304 | tf_op jit(solution)/shard_map/all_to_all | solution.py:216
  275.4 3.4 fusion.21
  279.7 1.3 fusion.18
  281.1 2.0 convert_multiply_fusion.4
  283.1 2.1 copy.186
  287.1 2.0 copy.187
  289.2 1.5 fusion.41
  291.4 1.3 fusion.17
  292.7 2.3 fusion.16
  295.0 1.3 fusion.15
  296.2 1.3 fusion.14
  299.7 2.5 all-to-all-done.1
  302.2 2.5 convert_select_fusion
  306.9 13.5 %scatter_fusion = f32[256,512]{1,0:T(8,128)S(1)} fusion(f32[256,512]{1,0:T(8,128)S(1)} %convolution_add_fusion.7, s32[2048]{0:T(1024)S(1)} %bitcast.259, f32[2048,512]{1,0:T(8,128)} %bitcast.218), kind=kCustom, calls=%fused_computation.3 | custom fusion | flops 1048576 | bytes 12591104 | tf_op jit(solution)/shard_map/scatter-add | solution.py:224
  320.6 65.8 %psum.15 = f32[512]{0:T(512)} all-reduce(f32[512]{0:T(512)S(1)} %get-tuple-element.245), channel_id=1, replica_groups=mesh['dom'=16,'blk'=8] {'dom','blk'}, use_global_device_ids=true, to_apply=%region_32.33 | all-reduce | flops 512 | bytes 4096 | tf_op jit(solution)/shard_map/psum | solution.py:242
  387.3 67.9 %all-reduce.2.cloned.1.call-done = f32[5,512,512]{2,1,0:T(8,128)} async-done(((f32[5,512,512]{2,1,0:T(8,128)}), f32[5,512,512]{2,1,0:T(8,128)}) %all-reduce.2.cloned.1.call-update) | async-done | bytes 5242896 | tf_op jit(solution)/shard_map/psum | solution.py:242
  455.3 5.8 %copy.248 = f32[5,512,512]{2,1,0:T(8,128)} copy(f32[5,512,512]{2,1,0:T(8,128)} %all-reduce.2.cloned.1.call-done) | data formatting | bytes 10485760
  (277 shorter events, 71.6 us)
Async XLA Ops:
  7.2 259.2 %copy-start = (bf16[512,512]{1,0:T(8,128)(2,1)S(1)}, bf16[512,512]{1,0:T(8,128)(2,1)}, u32[]{:S(2)}) copy-start(bf16[512,512]{1,0:T(8,128)(2,1)} %param.22) | copy-start | bytes 1572868
  7.2 34.3 %all-gather.6.cloned.1.call-start = ((), (), s32[]{:S(2)}) async-start(), calls=%async_computation.5 | async-start | bytes 2359296 | tf_op jit(solution)/shard_map/all_gather | solution.py:154
  10.8 1.5 copy-start.1
  11.0 1.3 copy-start.19
  11.1 2.3 copy-start.21
  11.4 2.1 copy-start.6
  12.3 56.8 %all-gather.4.cloned.1.call-start = ((), (), s32[]{:S(2)}) async-start(), calls=%async_computation.4 | async-start | bytes 2359296 | tf_op jit(solution)/shard_map/all_gather | solution.py:155
  13.4 267.7 %reduce-scatter.3.cloned.1.call-start = ((), (), s32[]{:S(2)}) async-start(), calls=%async_computation.6 | async-start | bytes 2359296 | tf_op jit(solution)/shard_map/reduce_scatter | solution.py:192
  14.0 3.1 copy-start.3
  14.0 4.3 copy-start.44
  14.0 17.5 %copy-start.49 = (s32[1,8]{1,0:T(1,128)S(1)}, s32[1,8]{1,0:T(1,128)}, u32[]{:S(2)}) copy-start(s32[1,8]{1,0:T(1,128)} %param.24) | copy-start | bytes 100
  14.1 19.2 %copy-start.7 = (bf16[256,512]{1,0:T(8,128)(2,1)S(1)}, bf16[256,512]{1,0:T(8,128)(2,1)}, u32[]{:S(2)}) copy-start(bf16[256,512]{1,0:T(8,128)(2,1)} %param.29) | copy-start | bytes 786436
  14.1 19.2 %copy-start.17 = (bf16[512,512]{1,0:T(8,128)(2,1)S(1)}, bf16[512,512]{1,0:T(8,128)(2,1)}, u32[]{:S(2)}) copy-start(bf16[512,512]{1,0:T(8,128)(2,1)} %param.21) | copy-start | bytes 1572868
  90.5 1.8 copy-start.24
  90.5 2.1 copy-start.37
  90.5 2.1 copy-start.43
  92.6 1.0 copy-start.36
  92.6 0.9 copy-start.42
  93.4 1.0 copy-start.35
  93.4 1.0 copy-start.41
  94.3 1.0 copy-start.34
  94.3 1.0 copy-start.40
  95.1 1.0 copy-start.33
  95.2 1.0 copy-start.39
  96.0 1.0 copy-start.32
  96.1 1.0 copy-start.38
  96.9 1.0 copy-start.31
  99.5 1.0 copy-start.23
  99.8 1.0 copy-start.30
  195.4 0.7 copy-start.45
  196.1 7.5 %copy-start.50 = (s32[16]{0:T(128)S(1)}, s32[16]{0:T(128)}, u32[]{:S(2)}) copy-start(s32[16]{0:T(128)} %param.26) | copy-start | bytes 196
  205.2 63.5 %all-to-all-start = ((bf16[16,128,512]{2,1,0:T(8,128)(2,1)}), bf16[16,128,512]{2,1,0:T(8,128)(2,1)}, u32[]{:S(2)}, u32[]{:S(2)}) async-start(bf16[16,128,512]{2,1,0:T(8,128)(2,1)} %broadcast_select_fusion), calls=%async_computation | async-start | bytes 4194304 | tf_op jit(solution)/shard_map/all_to_all | solution.py:131
  211.8 0.7 copy-start.47
  211.8 0.7 copy-start.48
  211.8 80.8 %reduce-scatter.5.cloned.1.call-start = ((), (), s32[]{:S(2)}) async-start(), calls=%async_computation.7 | async-start | bytes 2359296 | tf_op jit(solution)/shard_map/reduce_scatter | solution.py:198
  236.1 30.3 %copy-start.8 = (bf16[256,512]{1,0:T(8,128)(2,1)S(1)}, bf16[256,512]{1,0:T(8,128)(2,1)}, u32[]{:S(2)}) copy-start(bf16[256,512]{1,0:T(8,128)(2,1)} %param.29) | copy-start | bytes 786436
  237.5 31.2 %copy-start.25 = (bf16[2048,256]{1,0:T(8,128)(2,1)}, bf16[2048,256]{1,0:T(8,128)(2,1)S(1)}, u32[]{:S(2)}) copy-start(bf16[2048,256]{1,0:T(8,128)(2,1)S(1)} %convert_element_type.131) | copy-start | bytes 3145732
  268.8 33.4 %all-to-all-start.1 = ((bf16[16,128,512]{2,1,0:T(8,128)(2,1)}), bf16[16,128,512]{2,1,0:T(8,128)(2,1)S(1)}, u32[]{:S(2)}, u32[]{:S(2)}) async-start(bf16[16,128,512]{2,1,0:T(8,128)(2,1)} %bitcast.233), calls=%async_computation.3 | async-start | bytes 4194304 | tf_op jit(solution)/shard_map/all_to_all | solution.py:216
  275.4 179.9 %all-reduce.2.cloned.1.call-start = ((), (), s32[]{:S(2)}) async-start(), calls=%async_computation.8 | async-start | bytes 10485760 | tf_op jit(solution)/shard_map/psum | solution.py:242
  275.4 3.4 copy-start.4
  279.0 0.7 copy-start.11
  281.1 8.1 %copy-start.2 = (f32[256,512]{1,0:T(8,128)S(1)}, f32[256,512]{1,0:T(8,128)}, u32[]{:S(2)}) copy-start(f32[256,512]{1,0:T(8,128)} %copy-done.1) | copy-start | bytes 1572868
  290.6 0.7 copy-start.13
  291.4 3.6 copy-start.9
  291.4 3.6 copy-start.27
  292.7 3.6 copy-start.28
  297.5 0.9 copy-start.5
  297.5 1.0 copy-start.29
  299.7 5.1 %copy-start.12 = (bf16[256,8,64]{0,2,1:T(8,128)(2,1)S(1)}, bf16[256,8,64]{0,2,1:T(8,128)(2,1)}, u32[]{:S(2)}) copy-start(bf16[256,8,64]{0,2,1:T(8,128)(2,1)} %copy-done.11) | copy-start | bytes 786436
  302.2 2.5 copy-start.22
  302.2 2.9 copy-start.16
  302.2 2.9 copy-start.18
  304.7 1.4 copy-start.14
  304.7 1.4 copy-start.15
  304.7 1.8 copy-start.20
  304.7 1.8 copy-start.26
  306.9 13.6 %copy-start.46 = (f32[512]{0:T(512)S(1)}, f32[512]{0:T(512)}, u32[]{:S(2)}) copy-start(f32[512]{0:T(512)} %param.17) | copy-start | bytes 6148
  306.9 79.6 %copy-start.10 = (bf16[256,512]{1,0:T(8,128)(2,1)S(1)}, bf16[256,512]{1,0:T(8,128)(2,1)}, u32[]{:S(2)}) copy-start(bf16[256,512]{1,0:T(8,128)(2,1)} %param.29) | copy-start | bytes 786436
Sparse Core Ops, SparseCore 0:
  12.4 29.0 all-gather.5
  43.2 25.8 all-gather.3
  195.5 30.9 reduce-scatter.2
  228.8 32.8 reduce-scatter.4
  297.7 157.5 all-reduce.1
where the time goes:
time: 470 us; the launch traced here: 468 us
  waiting for transfers between devices  102 us (22%)
  local copies, waits for them, and re-layouts  97.6 us (21%)
  other arithmetic  84.2 us (18%)
  blocking collectives  78.9 us (17%)
  matrix products  70.8 us (15%)
  between operations  14.7 us (3%)
  starting transfers between devices  13.4 us (3%)
  loops' own time  5.81 us (1%)
    psum x1, waiting for transfers between devices, local(): weight_sums, gain_sum = lax.psum((weight_terms, gain_term), ('dom', 'blk'))  67.9 us
    psum x1, blocking collectives, local(): weight_sums, gain_sum = lax.psum((weight_terms, gain_term), ('dom', 'blk'))  65.8 us
    scatter-add x1, other arithmetic, local(): jax.ops.segment_sum(jnp.ones(edge_dst.shape, jnp.float32), edge_dst, row_...  28.8 us
    all_gather x1, waiting for transfers between devices, local(): lax.all_gather(value_flat, 'blk', axis=0, tiled=True)  23.3 us
    scatter-add x1, other arithmetic, local(): jnp.zeros((peer_count * slot_count * row_count,), jnp.int32).at[pair_index]  22.4 us
    unnamed x106, local copies, waits for them, and re-layouts  20.3 us
    dot_general x16, matrix products, block_weights(): jnp.einsum('rhe,khe->hrk', query_heads, key_heads, preferred_element_type...  19.7 us
    slice x9, local copies, waits for them, and re-layouts, attend_piece(): value_rows[first_row:last_row].reshape(part_rows, HEADS, HEAD_DIM)  13.6 us
  transfers between devices with their start and end apart: 7, of which 4 were waited for; matrix products, arithmetic and copies ran while one was open for 25% of the time, Pallas kernels for 0%

commit v1 on v0

--- a/solution.py
+++ b/solution.py
@@ -152,7 +152,9 @@
     key_set = None
     key_set = (
         lax.all_gather(key_flat, "blk", axis=0, tiled=True),
-        lax.all_gather(value_flat, "blk", axis=0, tiled=True),
+        jnp.concatenate(
+            lax.all_to_all(jnp.stack([value_flat] * lax.axis_size("blk")), "blk", 0, 0), axis=0
+        ),
         lax.all_gather(node_cluster, "blk", axis=0, tiled=True),
     )
     numer, denom = fold_step(start_state, key_set, 0)

time: 470 us -> 445 us (0.947)
  waiting for transfers between devices: 102 us -> 69.9 us
  local copies, waits for them, and re-layouts: 97.6 us -> 79.9 us
  blocking collectives: 78.9 us -> 92.2 us
  starting transfers between devices: 13.4 us -> 20.3 us
    all_gather x1 -> x0, waiting for transfers between devices: 23.3 us -> none  [local(): lax.all_gather(value_flat, 'blk', axis=0, tiled=True)]
    all_gather x1, blocking collectives: 13.1 us -> 26.4 us  [local(): lax.all_gather(node_cluster, 'blk', axis=0, tiled=True)]
    slice x9 -> x1, local copies, waits for them, and re-layouts: 13.6 us -> 1.36 us  [attend_piece(): value_rows[first_row:last_row].reshape(part_rows, HEADS, HEAD_DIM)]
    all_gather x1, waiting for transfers between devices: 7.86 us -> 0.01 us  [local(): lax.all_gather(key_flat, 'blk', axis=0, tiled=True)]
    all_to_all x0 -> x1, starting transfers between devices: none -> 6.81 us  [local(): lax.all_to_all(jnp.stack([value_flat] * lax.axis_size('blk')), 'blk', 0, 0)]
    reshape x1 -> x0, local copies, waits for them, and re-layouts: 6.14 us -> none  [local(): value_rows.reshape(block_count, row_count, HEADS, HEAD_DIM)]
    unnamed x106 -> x119, local copies, waits for them, and re-layouts: 20.3 us -> 16.1 us
  transfers between devices with their start and end apart: 7 -> 7, of which waited for: 4 -> 2; matrix products, arithmetic and copies ran while one was open for 25% -> 28% of each run, Pallas kernels for 0% -> 0%
where the time goes in v1:
time: 445 us; the launch traced here: 443 us
  blocking collectives  92.2 us (21%)
  other arithmetic  86.1 us (19%)
  local copies, waits for them, and re-layouts  79.9 us (18%)
  matrix products  73.9 us (17%)
  waiting for transfers between devices  69.9 us (16%)
  starting transfers between devices  20.3 us (5%)
  between operations  14.7 us (3%)
  loops' own time  5.81 us (1%)
    psum x1, waiting for transfers between devices, local(): weight_sums, gain_sum = lax.psum((weight_terms, gain_term), ('dom', 'blk'))  66.1 us
    psum x1, blocking collectives, local(): weight_sums, gain_sum = lax.psum((weight_terms, gain_term), ('dom', 'blk'))  65.8 us
    scatter-add x1, other arithmetic, local(): jax.ops.segment_sum(jnp.ones(edge_dst.shape, jnp.float32), edge_dst, row_...  28.8 us
    all_gather x1, blocking collectives, local(): lax.all_gather(node_cluster, 'blk', axis=0, tiled=True)  26.4 us
    scatter-add x1, other arithmetic, local(): jnp.zeros((peer_count * slot_count * row_count,), jnp.int32).at[pair_index]  22.4 us
    dot_general x16, matrix products, block_weights(): jnp.einsum('rhe,khe->hrk', query_heads, key_heads, preferred_element_type...  19.7 us
    unnamed x119, local copies, waits for them, and re-layouts  16.1 us
    scatter-add x1, other arithmetic, local(): jax.ops.segment_sum(returned.reshape(peer_count * slot_count, feat_width)...  13.7 us
  transfers between devices with their start and end apart: 7, of which 2 were waited for; matrix products, arithmetic and copies ran while one was open for 28% of the time, Pallas kernels for 0%

profile of v1, /device:TPU:1, one launch (start us, length us, event | category | flops | bytes accessed | tf_op | source)
XLA Modules:
  0.0 442.7 jit_solution(4552694515817896444)
XLA Ops:
  9.5 1.3 fusion.57
  12.7 1.5 stack.14
  14.2 6.8 %all-to-all-start.1 = ((bf16[8,256,512]{1,2,0:T(8,128)(2,1)}), bf16[8,256,512]{1,2,0:T(8,128)(2,1)S(1)}, u32[]{:S(2)}, u32[]{:S(2)}) async-start(bf16[8,256,512]{1,2,0:T(8,128)(2,1)} %stack.14), calls=%async_computation.1 | async-start | bytes 4194304 | tf_op jit(solution)/shard_map/all_to_all | solution.py:156
  21.0 2.2 fusion.66
  23.1 2.0 copy.125
  27.1 2.0 copy.126
  29.2 2.0 multiply_convert_fusion.1
  31.2 1.8 copy.127
  33.0 26.4 %all-gather = s32[8,1,256]{2,1,0:T(1,128)S(1)} all-gather(s32[1,1,256]{2,1,0:T(1,128)S(1)} %bitcast.260), channel_id=1, replica_groups=mesh['dom'=16,'blk'=8] {'blk'}, dimensions={0}, use_global_device_ids=true | all-gather | bytes 9216 | tf_op jit(solution)/shard_map/all_gather | solution.py:158
  59.6 1.5 compare_and_fusion.1
  61.2 2.3 fusion.67
  63.5 1.4 fusion.55
  64.8 2.9 fusion.54
  67.8 1.9 copy.130
  69.7 1.8 copy.132
  71.5 1.8 copy.134
  73.3 1.8 copy.136
  77.1 1.7 fusion.64
  89.5 6.1 %reshape.809 = bf16[8,256,8,64]{3,2,1,0:T(8,128)(2,1)} reshape(bf16[2048,512]{1,0:T(8,128)(2,1)} %all-gather.3.cloned.1.call-done) | data formatting | bytes 4194304 | tf_op jit(solution)/shard_map/reshape | solution.py:184
  95.6 5.1 %copy.148 = bf16[8,256,8,64]{1,3,2,0:T(8,128)(2,1)} copy(bf16[8,256,8,64]{3,2,1,0:T(8,128)(2,1)} %reshape.809) | data formatting | bytes 4194304
  100.7 66.8 %while.17 = (s32[]{:T(128)}, f32[256,8,64]{0,2,1:T(8,128)S(1)}, bf16[8,256,512]{1,2,0:T(8,128)(2,1)}, bf16[8,256,512]{2,1,0:T(8,128)(2,1)}, bf16[8,256,8,64]{1,3...) while((s32[]{:T(128)}, f32[256,8,64]{0,2,1:T(8,128)S(1)}, ...), condition=%wide.region_23.24_spmd.clone, body=%wide.region_22.23_spmd.clone.sunk | while | flops 340262912 | bytes 15088305 | solution.py:190
  102.1 1.6 bitcast_select_fusion.2
  103.7 1.4 fusion.163
  107.7 1.2 fusion.164
  110.5 1.6 bitcast_select_fusion.2
  112.1 1.4 fusion.163
  118.8 1.6 bitcast_select_fusion.2
  120.4 1.4 fusion.163
  127.2 1.6 bitcast_select_fusion.2
  128.8 1.4 fusion.163
  135.5 1.6 bitcast_select_fusion.2
  137.1 1.4 fusion.163
  143.9 1.6 bitcast_select_fusion.2
  145.5 1.4 fusion.163
  149.4 1.2 fusion.164
  152.3 1.6 bitcast_select_fusion.2
  153.9 1.4 fusion.163
  160.6 1.6 bitcast_select_fusion.2
  162.2 1.4 fusion.163
  167.6 4.0 copy.149
  172.3 7.5 %gather_fusion = bf16[2048,512]{1,0:T(8,128)(2,1)S(1)} fusion(bf16[256,512]{1,0:T(8,128)(2,1)S(1)} %fusion.38, s32[2048]{0:T(1024)S(1)} %fusion.48), kind=kCustom, calls=%fused_computation | custom fusion | bytes 4202496 | tf_op jit(solution)/shard_map/gather | solution.py:130
  179.9 1.5 broadcast_select_fusion
  181.4 6.8 %all-to-all-start = ((bf16[16,128,512]{2,1,0:T(8,128)(2,1)}), bf16[16,128,512]{2,1,0:T(8,128)(2,1)}, u32[]{:S(2)}, u32[]{:S(2)}) async-start(bf16[16,128,512]{2,1,0:T(8,128)(2,1)} %broadcast_select_fusion), calls=%async_computation | async-start | bytes 4194304 | tf_op jit(solution)/shard_map/all_to_all | solution.py:131
  189.0 22.4 %scatter_custom_fusion = s32[524288]{0:T(1024)S(1)} fusion(s32[4096]{0:T(1024)S(1)} %compare_select_fusion, s32[4096]{0:T(1024)S(1)} %broadcast.738, s32[]{:T(128)} %constant.148.clone.1), kind=kCustom, calls=%fused_computation.77 | custom fusion | flops 4096 | bytes 2097156 | tf_op jit(solution)/shard_map/scatter-add | solution.py:163
  212.6 1.5 convert_element_type.131
  214.0 28.8 %scatter_custom_fusion.1 = f32[256]{0:T(256)S(1)} fusion(s32[4096]{0:T(1024)S(1)} %copy-done.55, f32[4096]{0:T(1024)S(1)} %broadcast.739, f32[]{:T(128)} %constant.152.clone.1), kind=kCustom, calls=%fused_computation.188 | custom fusion | flops 4096 | bytes 1028 | tf_op jit(solution)/shard_map/scatter-add | solution.py:166
  242.8 2.4 convolution_convert_fusion
  245.2 6.6 %all-to-all-start.2 = ((bf16[16,128,512]{2,1,0:T(8,128)(2,1)}), bf16[16,128,512]{2,1,0:T(8,128)(2,1)S(1)}, u32[]{:S(2)}, u32[]{:S(2)}) async-start(bf16[16,128,512]{2,1,0:T(8,128)(2,1)} %bitcast.235), calls=%async_computation.4 | async-start | bytes 4194304 | tf_op jit(solution)/shard_map/all_to_all | solution.py:218
  251.9 3.4 fusion.21
  256.2 1.3 fusion.18
  257.5 2.1 convert_multiply_fusion.4
  259.6 2.1 copy.151
  263.6 2.1 copy.152
  265.7 1.5 fusion.41
  267.9 1.3 fusion.17
  269.2 2.3 fusion.16
  271.5 1.3 fusion.15
  272.7 1.3 fusion.14
  276.1 3.0 all-to-all-done.2
  279.2 2.3 convert_select_fusion
  283.7 13.7 %scatter_fusion = f32[256,512]{1,0:T(8,128)S(1)} fusion(f32[256,512]{1,0:T(8,128)S(1)} %convolution_add_fusion.7, s32[2048]{0:T(1024)S(1)} %bitcast.261, f32[2048,512]{1,0:T(8,128)} %bitcast.219), kind=kCustom, calls=%fused_computation.3 | custom fusion | flops 1048576 | bytes 12591104 | tf_op jit(solution)/shard_map/scatter-add | solution.py:226
  297.6 65.8 %psum.15 = f32[512]{0:T(512)} all-reduce(f32[512]{0:T(512)S(1)} %get-tuple-element.245), channel_id=1, replica_groups=mesh['dom'=16,'blk'=8] {'dom','blk'}, use_global_device_ids=true, to_apply=%region_32.33 | all-reduce | flops 512 | bytes 4096 | tf_op jit(solution)/shard_map/psum | solution.py:244
  364.3 66.1 %all-reduce.2.cloned.1.call-done = f32[5,512,512]{2,1,0:T(8,128)} async-done(((f32[5,512,512]{2,1,0:T(8,128)}), f32[5,512,512]{2,1,0:T(8,128)}) %all-reduce.2.cloned.1.call-update) | async-done | bytes 5242896 | tf_op jit(solution)/shard_map/psum | solution.py:244
  430.4 5.8 %copy.211 = f32[5,512,512]{2,1,0:T(8,128)} copy(f32[5,512,512]{2,1,0:T(8,128)} %all-reduce.2.cloned.1.call-done) | data formatting | bytes 10485760
  (282 shorter events, 64.3 us)
Async XLA Ops:
  7.2 235.7 %copy-start = (bf16[512,512]{1,0:T(8,128)(2,1)S(1)}, bf16[512,512]{1,0:T(8,128)(2,1)}, u32[]{:S(2)}) copy-start(bf16[512,512]{1,0:T(8,128)(2,1)} %param.22) | copy-start | bytes 1572868
  7.2 57.7 %all-gather.3.cloned.1.call-start = ((), (), s32[]{:S(2)}) async-start(), calls=%async_computation.5 | async-start | bytes 2359296 | tf_op jit(solution)/shard_map/all_gather | solution.py:154
  10.8 1.4 copy-start.3
  11.0 1.2 copy-start.18
  11.3 2.8 copy-start.7
  14.2 49.3 %all-to-all-start.1 = ((bf16[8,256,512]{1,2,0:T(8,128)(2,1)}), bf16[8,256,512]{1,2,0:T(8,128)(2,1)S(1)}, u32[]{:S(2)}, u32[]{:S(2)}) async-start(bf16[8,256,512]{1,2,0:T(8,128)(2,1)} %stack.14), calls=%async_computation.1 | async-start | bytes 4194304 | tf_op jit(solution)/shard_map/all_to_all | solution.py:156
  21.0 236.6 %reduce-scatter.3.cloned.1.call-start = ((), (), s32[]{:S(2)}) async-start(), calls=%async_computation.6 | async-start | bytes 2359296 | tf_op jit(solution)/shard_map/reduce_scatter | solution.py:194
  25.2 7.8 %copy-start.51 = (s32[256]{0:T(256)S(1)}, s32[256]{0:T(256)}, u32[]{:S(2)}) copy-start(s32[256]{0:T(256)} %param.23) | copy-start | bytes 3076
  25.2 34.3 %copy-start.56 = (s32[1,8]{1,0:T(1,128)S(1)}, s32[1,8]{1,0:T(1,128)}, u32[]{:S(2)}) copy-start(s32[1,8]{1,0:T(1,128)} %param.24) | copy-start | bytes 100
  63.5 4.3 copy-start.1
  67.7 7.4 %copy-start.32 = (bf16[256,512]{1,0:T(8,128)(2,1)S(1)}, bf16[256,512]{1,0:T(8,128)(2,1)}, u32[]{:S(2)}) copy-start(bf16[256,512]{1,0:T(8,128)(2,1)} %get-tuple-element.282) | copy-start | bytes 786436
  67.7 8.2 %copy-start.31 = (bf16[256,512]{1,0:T(8,128)(2,1)S(1)}, bf16[256,512]{1,0:T(8,128)(2,1)}, u32[]{:S(2)}) copy-start(bf16[256,512]{1,0:T(8,128)(2,1)} %get-tuple-element.281) | copy-start | bytes 786436
  67.7 9.1 %copy-start.30 = (bf16[256,512]{1,0:T(8,128)(2,1)S(1)}, bf16[256,512]{1,0:T(8,128)(2,1)}, u32[]{:S(2)}) copy-start(bf16[256,512]{1,0:T(8,128)(2,1)} %get-tuple-element.280) | copy-start | bytes 786436
  67.8 9.2 %copy-start.29 = (bf16[256,512]{1,0:T(8,128)(2,1)S(1)}, bf16[256,512]{1,0:T(8,128)(2,1)}, u32[]{:S(2)}) copy-start(bf16[256,512]{1,0:T(8,128)(2,1)} %get-tuple-element.279) | copy-start | bytes 786436
  67.8 9.3 %copy-start.2 = (bf16[256,512]{0,1:T(8,128)(2,1)S(1)}, bf16[256,512]{0,1:T(8,128)(2,1)}, u32[]{:S(2)}) copy-start(bf16[256,512]{0,1:T(8,128)(2,1)} %copy.127) | copy-start | bytes 786436
  76.9 1.9 copy-start.28
  77.1 2.1 copy-start.44
  77.1 2.1 copy-start.50
  79.2 1.0 copy-start.43
  79.2 0.9 copy-start.49
  80.0 1.0 copy-start.42
  80.0 1.0 copy-start.48
  80.9 1.0 copy-start.41
  80.9 1.0 copy-start.47
  81.7 1.0 copy-start.40
  81.7 1.0 copy-start.46
  82.6 0.9 copy-start.45
  84.3 1.0 copy-start.27
  85.0 1.0 copy-start.26
  85.2 1.1 copy-start.25
  86.0 1.0 copy-start.24
  86.3 1.0 copy-start.23
  87.0 1.0 copy-start.22
  87.3 1.1 copy-start.21
  87.3 1.1 copy-start.39
  172.3 7.5 %copy-start.57 = (s32[16]{0:T(128)S(1)}, s32[16]{0:T(128)}, u32[]{:S(2)}) copy-start(s32[16]{0:T(128)} %param.26) | copy-start | bytes 196
  181.4 63.8 %all-to-all-start = ((bf16[16,128,512]{2,1,0:T(8,128)(2,1)}), bf16[16,128,512]{2,1,0:T(8,128)(2,1)}, u32[]{:S(2)}, u32[]{:S(2)}) async-start(bf16[16,128,512]{2,1,0:T(8,128)(2,1)} %broadcast_select_fusion), calls=%async_computation | async-start | bytes 4194304 | tf_op jit(solution)/shard_map/all_to_all | solution.py:131
  188.2 0.8 copy-start.54
  188.2 0.8 copy-start.55
  188.3 80.9 %reduce-scatter.5.cloned.1.call-start = ((), (), s32[]{:S(2)}) async-start(), calls=%async_computation.7 | async-start | bytes 2359296 | tf_op jit(solution)/shard_map/reduce_scatter | solution.py:200
  212.6 30.3 %copy-start.8 = (bf16[256,512]{1,0:T(8,128)(2,1)S(1)}, bf16[256,512]{1,0:T(8,128)(2,1)}, u32[]{:S(2)}) copy-start(bf16[256,512]{1,0:T(8,128)(2,1)} %param.29) | copy-start | bytes 786436
  214.0 31.2 %copy-start.33 = (bf16[2048,256]{1,0:T(8,128)(2,1)}, bf16[2048,256]{1,0:T(8,128)(2,1)S(1)}, u32[]{:S(2)}) copy-start(bf16[2048,256]{1,0:T(8,128)(2,1)S(1)} %convert_element_type.131) | copy-start | bytes 3145732
  245.2 34.0 %all-to-all-start.2 = ((bf16[16,128,512]{2,1,0:T(8,128)(2,1)}), bf16[16,128,512]{2,1,0:T(8,128)(2,1)S(1)}, u32[]{:S(2)}, u32[]{:S(2)}) async-start(bf16[16,128,512]{2,1,0:T(8,128)(2,1)} %bitcast.235), calls=%async_computation.4 | async-start | bytes 4194304 | tf_op jit(solution)/shard_map/all_to_all | solution.py:218
  251.9 178.5 %all-reduce.2.cloned.1.call-start = ((), (), s32[]{:S(2)}) async-start(), calls=%async_computation.8 | async-start | bytes 10485760 | tf_op jit(solution)/shard_map/psum | solution.py:244
  251.9 3.4 copy-start.5
  255.5 0.7 copy-start.11
  257.5 8.1 %copy-start.4 = (f32[256,512]{1,0:T(8,128)S(1)}, f32[256,512]{1,0:T(8,128)}, u32[]{:S(2)}) copy-start(f32[256,512]{1,0:T(8,128)} %copy-done.3) | copy-start | bytes 1572868
  267.2 0.7 copy-start.13
  267.9 3.6 copy-start.9
  267.9 3.6 copy-start.35
  269.2 3.6 copy-start.37
  274.0 0.9 copy-start.6
  274.0 1.0 copy-start.38
  276.1 5.4 %copy-start.12 = (bf16[256,8,64]{0,2,1:T(8,128)(2,1)S(1)}, bf16[256,8,64]{0,2,1:T(8,128)(2,1)}, u32[]{:S(2)}) copy-start(bf16[256,8,64]{0,2,1:T(8,128)(2,1)} %copy-done.11) | copy-start | bytes 786436
  279.2 2.3 copy-start.20
  279.2 2.7 copy-start.16
  279.2 2.7 copy-start.17
  279.2 2.7 copy-start.36
  281.5 1.5 copy-start.14
  281.5 1.5 copy-start.15
  281.5 1.8 copy-start.19
  281.5 1.8 copy-start.34
  283.7 13.7 %copy-start.53 = (f32[512]{0:T(512)S(1)}, f32[512]{0:T(512)}, u32[]{:S(2)}) copy-start(f32[512]{0:T(512)} %param.17) | copy-start | bytes 6148
  283.7 79.7 %copy-start.10 = (bf16[256,512]{1,0:T(8,128)(2,1)S(1)}, bf16[256,512]{1,0:T(8,128)(2,1)}, u32[]{:S(2)}) copy-start(bf16[256,512]{1,0:T(8,128)(2,1)} %param.29) | copy-start | bytes 786436
  (1 other events, 0.7 us)
Sparse Core Ops, SparseCore 0:
  12.4 37.7 all-gather.2
  171.7 30.0 reduce-scatter.2
  204.2 32.7 reduce-scatter.4
  274.2 156.1 all-reduce.1
